TPU v7x, 32 devices: a whole 2x2x4 slice. The times are simulated.
32 devices in a mesh: grp: 2 (over y), head: 4 (over z), tm: 4 (over x, core).
Axes of the slice: x: 2, y: 2, z: 4, core: 2. Of those that a mesh axis runs over, the one named last changes fastest.
Arguments:
- query_rows: bfloat16 [32, 64, 3072], P(('grp', 'tm'), 'head'), parts along dimension 0, may hold values from -180 to 180
- key_rows: bfloat16 [32, 64, 3072], P(('grp', 'tm'), 'head'), parts along dimension 0, may hold values from -6 to 6
- value_rows: bfloat16 [32, 64, 3072], P(('grp', 'tm'), 'head'), parts along dimension 0, may hold values from -6 to 6
- pair_list: int32 [32, 32], P('grp'), parts along dimension 0, may hold values from 0 to 15, as said below
- block_tokens: int32 [32], P('grp'), parts along dimension 0, may hold values from 1 to 64, 768 in all
Outputs:
- attended: bfloat16 [32, 64, 3072], P(('grp', 'tm'), 'head'), parts along dimension 0
There are 2 independent parts, one for each index of `grp`. A program takes and returns all parts, laid end to end along the dimension named above; each array names one. Nothing has to cross between parts.
Inputs may be any that keep to these rules, and one draw needn't show every extreme that they name: `pair_list`: row q names q in column 0 and q xor 1 in column 1; a block may be named twice in a row. The query blocks of one time shard name at most 2 different blocks of a time shard beside it and at most 1 of a time shard two or more away; both bounds are reached.
All inputs are finite; a program needn't handle non-finite values.
Results may differ from a plain program's by a relative error of at most 0.0012.
The roundings to bfloat16 on the way count: a program that leaves them out, or rounds other values in their place, can miss the bound.
Values may be sent and summed in bfloat16 or wider, within the bound.
A program may use at most 128 MiB of HBM per device.

v0:
```python
import functools
import math

import jax
import jax.numpy as jnp
from jax import lax
from jax.experimental import pallas as pl
from jax.experimental.pallas import tpu as pltpu
from jax.sharding import PartitionSpec as P

HD = 128
NEAR_CAP = 2
FAR_CAP = 1
LANES = 128
MESH = pl.DeviceIdType.MESH


def incoming_slots(count_tm):
    slots = []
    for offset in range(1, count_tm):
        capacity = NEAR_CAP if offset in (1, count_tm - 1) else FAR_CAP
        slots += [(offset, place) for place in range(capacity)]
    return slots


def sign_table(dimension):
    rows = lax.broadcasted_iota(jnp.int32, (dimension, dimension), 0)
    columns = lax.broadcasted_iota(jnp.int32, (dimension, dimension), 1)
    common = rows & columns
    parity = jnp.zeros((dimension, dimension), jnp.int32)
    for bit_level in range(dimension.bit_length() - 1):
        parity = parity + ((common >> bit_level) & 1)
    return jnp.where((parity & 1) == 0, 1.0, -1.0).astype(jnp.float32)


def kernel(
    sizes,
    query_ref,
    key_ref,
    value_ref,
    pair_ref,
    tokens_ref,
    out_ref,
    gathered,
    store,
    outbox,
    staged,
    pair_here,
    listed_ref,
    place_ref,
    wanted_ref,
    bias_ref,
    sign_ref,
    head_send,
    head_recv,
    local_sem,
    halo_send,
    halo_recv,
    back_send,
    back_recv,
    back_local,
    pair_sem,
):
    count_head, count_tm, blocks, part, heads, block, total_blocks, slots, padded = sizes
    width = heads * HD
    my_head = lax.axis_index("head")
    me = lax.axis_index("tm")
    scale = 1.0 / math.sqrt(HD)
    slot_of = {slot: i for i, slot in enumerate(slots)}
    sources = (key_ref, value_ref, query_ref)

    for offset in range(1, count_head):
        peer = lax.rem(my_head + offset, count_head)
        pl.semaphore_signal(
            pltpu.get_barrier_semaphore(), inc=1, device_id={"head": peer}, device_id_type=MESH
        )

    def columns_of(owner, h):
        return pl.ds(pl.multiple_of(owner * width + h * HD, HD), HD)

    def head_copy(which, offset, h):
        peer = lax.rem(my_head + offset, count_head)
        return pltpu.make_async_remote_copy(
            src_ref=sources[which].at[:, :, columns_of(peer, h)],
            dst_ref=gathered.at[which, h, my_head],
            send_sem=head_send.at[which, offset - 1, h],
            recv_sem=head_recv.at[which, offset - 1, h],
            device_id={"head": peer},
            device_id_type=MESH,
        )

    def local_copy(which, h):
        return pltpu.make_async_copy(
            sources[which].at[:, :, columns_of(my_head, h)],
            gathered.at[which, h, my_head],
            local_sem.at[which, h],
        )

    def halo_copy(which, h, slot):
        offset, place = slot
        peer = lax.rem(me + offset, count_tm)
        landing = slot_of[(count_tm - offset, place)]
        return pltpu.make_async_remote_copy(
            src_ref=outbox.at[which, h, slot_of[slot]],
            dst_ref=store.at[which, h, blocks + landing],
            send_sem=halo_send.at[which, h, slot_of[slot]],
            recv_sem=halo_recv.at[which, h, landing],
            device_id={"tm": peer},
            device_id_type=MESH,
        )

    def halo_arrival(which, h, slot):
        i = slot_of[slot]
        peer = lax.rem(me + slot[0], count_tm)
        return pltpu.make_async_remote_copy(
            src_ref=outbox.at[which, h, i],
            dst_ref=store.at[which, h, blocks + i],
            send_sem=halo_send.at[which, h, i],
            recv_sem=halo_recv.at[which, h, i],
            device_id={"tm": peer},
            device_id_type=MESH,
        )

    def if_used(slot, action):
        if slot[1] < FAR_CAP:
            action()
        else:
            peer = lax.rem(me + slot[0], count_tm)
            near = (peer == me + 1) | (peer == me - 1)
            pl.when(near)(action)

    def back_copy(offset, h):
        peer = lax.rem(my_head + offset, count_head)
        return pltpu.make_async_remote_copy(
            src_ref=staged.at[h, peer],
            dst_ref=out_ref.at[:, :, columns_of(my_head, h)],
            send_sem=back_send.at[offset - 1, h],
            recv_sem=back_recv.at[offset - 1, h],
            device_id={"head": peer},
            device_id_type=MESH,
        )

    def back_own(h):
        return pltpu.make_async_copy(
            staged.at[h, my_head],
            out_ref.at[:, :, columns_of(my_head, h)],
            back_local.at[h],
        )

    store[:, :, blocks:] = jnp.zeros((2, heads, padded - blocks, block, HD), jnp.bfloat16)
    for offset in range(1, count_tm):
        peer = lax.rem(me + offset, count_tm)
        pl.semaphore_signal(
            pltpu.get_barrier_semaphore(), inc=1, device_id={"tm": peer}, device_id_type=MESH
        )
    pair_copy = pltpu.make_async_copy(pair_ref, pair_here, pair_sem)
    pair_copy.start()
    for which in range(3):

        def start_local(h, carry, which=which):
            local_copy(which, h).start()
            return carry

        lax.fori_loop(0, heads, start_local, 0)
    sign_ref[...] = sign_table(HD).astype(jnp.bfloat16)
    pl.semaphore_wait(pltpu.get_barrier_semaphore(), count_head - 1 + count_tm - 1)
    for which in range(3):

        def start_remote(h, carry, which=which):
            for offset in range(1, count_head):
                head_copy(which, offset, h).start()
            return carry

        lax.fori_loop(0, heads, start_remote, 0)

    pair_copy.wait()
    pairs = pair_here[...]
    lane = lax.broadcasted_iota(jnp.int32, (1, LANES), 1)
    listed = jnp.zeros((total_blocks, LANES), jnp.float32)
    token_row = jnp.zeros((1, LANES), jnp.float32)
    for k in range(total_blocks):
        found = jnp.max(jnp.where(pairs == k, 1.0, 0.0), axis=1, keepdims=True)
        here = jnp.where(lane == k, 1.0, 0.0)
        listed = listed + found * here
        token_row = token_row + here * tokens_ref[k].astype(jnp.float32)
    wanted_ref[...] = jnp.zeros_like(wanted_ref)
    for t in range(count_tm):
        of_shard = listed[t * blocks : (t + 1) * blocks]
        listed_ref[t] = of_shard
        wanted_ref[t : t + 1, :] = jnp.max(of_shard, axis=0, keepdims=True)
    low = lax.broadcasted_iota(jnp.int32, (LANES, LANES), 0)
    high = lax.broadcasted_iota(jnp.int32, (LANES, LANES), 1)
    low_shard, high_shard = jnp.zeros_like(low), jnp.zeros_like(high)
    lane_shard = jnp.zeros_like(lane)
    for t in range(1, count_tm):
        low_shard = low_shard + jnp.where(low >= t * blocks, 1, 0)
        high_shard = high_shard + jnp.where(high >= t * blocks, 1, 0)
        lane_shard = lane_shard + jnp.where(lane >= t * blocks, 1, 0)
    before = jnp.where((low_shard == high_shard) & (low < high), 1.0, 0.0).astype(jnp.bfloat16)
    wanted = wanted_ref[...]
    rank = jnp.dot(wanted.astype(jnp.bfloat16), before, preferred_element_type=jnp.float32)
    for place in range(NEAR_CAP):
        chosen = jnp.where(rank == float(place), wanted, 0.0)
        for t in range(count_tm):
            place_ref[place, t] = chosen[t : t + 1, :]
    picks = []
    for offset, place in slots:
        row = place_ref[place, lax.rem(me + offset, count_tm)]
        picks.append(
            [
                jnp.sum(jnp.where(lane == me * blocks + j, row, 0.0), axis=1, keepdims=True)
                for j in range(blocks)
            ]
        )
    mine = listed_ref[me]
    key_lane = lax.broadcasted_iota(jnp.int32, (1, padded * block), 1)
    key_end = jnp.zeros((blocks, padded * block), jnp.float32)
    for i in range(blocks + len(slots)):
        if i < blocks:
            kept_tokens = jnp.where(lane == me * blocks + i, token_row, 0.0)
        else:
            offset, place = slots[i - blocks]
            owner = lax.rem(me + offset, count_tm)
            row = place_ref[place, me]
            kept_tokens = jnp.where(lane_shard == owner, row * token_row, 0.0)
        kept = jnp.sum(mine * kept_tokens, axis=1, keepdims=True)
        inside = jnp.where((key_lane >= i * block) & (key_lane < (i + 1) * block), 1.0, 0.0)
        key_end = key_end + inside * (kept + float(i * block))
    bias_ref[...] = jnp.where(key_lane.astype(jnp.float32) < key_end, 0.0, -1e30)

    def arrived(which, h):
        local_copy(which, h).wait()
        for offset in range(1, count_head):
            head_copy(which, offset, h).wait_recv()
        rows = jnp.concatenate(
            [
                gathered[which, h, :, b].astype(jnp.float32).reshape(block, HD)
                for b in range(blocks)
            ],
            axis=0,
        ).astype(jnp.bfloat16)
        turned = jnp.dot(rows, sign_ref[...], preferred_element_type=jnp.float32) * scale
        return turned.astype(jnp.bfloat16)

    for which in range(2):

        def spread(h, carry, which=which):
            turned = arrived(which, h)
            store[which, h, 0:blocks] = turned.reshape(blocks, block, HD)
            wide = turned.astype(jnp.float32)
            for i, slot in enumerate(slots):
                sent = picks[i][0] * wide[0:block]
                for j in range(1, blocks):
                    sent = sent + picks[i][j] * wide[j * block : (j + 1) * block]
                outbox[which, h, i] = sent.astype(jnp.bfloat16)
            for slot in slots:
                if_used(slot, lambda slot=slot: halo_copy(which, h, slot).start())
            return carry

        lax.fori_loop(0, heads, spread, 0)

    position = lax.broadcasted_iota(jnp.int32, (block, HD), 0)

    def attend(h, carry):
        query = arrived(2, h)
        for which in range(2):
            for slot in slots:
                if_used(slot, lambda slot=slot, which=which: halo_arrival(which, h, slot).wait_recv())
        keys = store[0, h].reshape(padded * block, HD)
        values = store[1, h].reshape(padded * block, HD)
        mixed = []
        for b in range(blocks):
            scores = lax.dot_general(
                query[b * block : (b + 1) * block],
                keys,
                (((1,), (1,)), ((), ())),
                preferred_element_type=jnp.float32,
            )
            scores = scores * scale + bias_ref[b : b + 1, :]
            peak = jnp.max(scores, axis=1, keepdims=True)
            weights = jnp.exp(scores - peak)
            denominator = jnp.sum(weights, axis=1, keepdims=True)
            total = jnp.dot(
                weights.astype(jnp.bfloat16), values, preferred_element_type=jnp.float32
            )
            mixed.append(total / denominator)
        mixed = jnp.concatenate(mixed, axis=0)
        first = mixed.astype(jnp.bfloat16)
        rest = mixed - first.astype(jnp.float32)
        second = rest.astype(jnp.bfloat16)
        third = (rest - second.astype(jnp.float32)).astype(jnp.bfloat16)
        sign = sign_ref[...]
        turned = jnp.dot(first, sign, preferred_element_type=jnp.float32)
        turned = turned + jnp.dot(second, sign, preferred_element_type=jnp.float32)
        turned = turned + jnp.dot(third, sign, preferred_element_type=jnp.float32)
        turned = turned * scale
        for b in range(blocks):
            live = position < tokens_ref[me * blocks + b]
            result = jnp.where(live, turned[b * block : (b + 1) * block], 0.0)
            for owner in range(count_head):
                staged[h, owner, b] = result[owner * part : (owner + 1) * part].astype(jnp.bfloat16)
        for offset in range(1, count_head):
            back_copy(offset, h).start()
        back_own(h).start()
        return carry

    lax.fori_loop(0, heads, attend, 0)

    def finish(h, carry):
        for which in range(3):
            for offset in range(1, count_head):
                head_copy(which, offset, h).wait_send()
        for which in range(2):
            for slot in slots:
                if_used(slot, lambda slot=slot, which=which: halo_copy(which, h, slot).wait_send())
        for offset in range(1, count_head):
            back_copy(offset, h).wait()
        back_own(h).wait()
        return carry

    lax.fori_loop(0, heads, finish, 0)


def shards(query_rows, key_rows, value_rows, pair_list, block_tokens):
    count_head = lax.axis_size("head")
    count_tm = lax.axis_size("tm")
    blocks, part, full_width = query_rows.shape
    block = part * count_head
    heads = full_width // (HD * count_head)
    total_blocks, listed = pair_list.shape
    slots = incoming_slots(count_tm)
    filled = blocks + len(slots)
    per_lane_tile = max(1, LANES // block)
    padded = -(-filled // per_lane_tile) * per_lane_tile
    shard_rows = -(-count_tm // 8) * 8
    sizes = (count_head, count_tm, blocks, part, heads, block, total_blocks, slots, padded)
    peers = max(1, count_head - 1)
    anywhere = pl.BlockSpec(memory_space=pl.ANY)
    dma = pltpu.SemaphoreType.DMA
    return pl.pallas_call(
        functools.partial(kernel, sizes),
        out_shape=jax.ShapeDtypeStruct(query_rows.shape, jnp.bfloat16),
        in_specs=[anywhere] * 4 + [pl.BlockSpec(memory_space=pltpu.SMEM)],
        out_specs=anywhere,
        scratch_shapes=[
            pltpu.VMEM((3, heads, count_head, blocks, part, HD), jnp.bfloat16),
            pltpu.VMEM((2, heads, padded, block, HD), jnp.bfloat16),
            pltpu.VMEM((2, heads, len(slots), block, HD), jnp.bfloat16),
            pltpu.VMEM((heads, count_head, blocks, part, HD), jnp.bfloat16),
            pltpu.VMEM((total_blocks, listed), jnp.int32),
            pltpu.VMEM((count_tm, blocks, LANES), jnp.float32),
            pltpu.VMEM((NEAR_CAP, count_tm, 1, LANES), jnp.float32),
            pltpu.VMEM((shard_rows, LANES), jnp.float32),
            pltpu.VMEM((blocks, padded * block), jnp.float32),
            pltpu.VMEM((HD, HD), jnp.bfloat16),
            dma((3, peers, heads)),
            dma((3, peers, heads)),
            dma((3, heads)),
            dma((2, heads, len(slots))),
            dma((2, heads, len(slots))),
            dma((peers, heads)),
            dma((peers, heads)),
            dma((heads,)),
            dma(()),
        ],
        compiler_params=pltpu.CompilerParams(
            collective_id=0, has_side_effects=True, vmem_limit_bytes=32 * 1024 * 1024
        ),
    )(query_rows, key_rows, value_rows, pair_list, block_tokens)


def solution(mesh):
    placed = (
        P(("grp", "tm"), "head", None),
        P(("grp", "tm"), "head", None),
        P(("grp", "tm"), "head", None),
        P("grp", None),
        P("grp"),
    )
    return jax.shard_map(
        shards,
        mesh=mesh,
        in_specs=placed,
        out_specs=P(("grp", "tm"), "head", None),
        check_vma=False,
    )
```

profile of v0, /device:TPU:0, one launch (start us, length us, event | category | flops | bytes accessed | tf_op | source)
XLA Modules:
  0.0 51.9 jit_solution(179602845578116922)
XLA Ops:
  0.0 0.0 copy-start
  0.0 1.0 %copy-done = bf16[4,16,3072]{2,1,0:T(8,128)(2,1)S(1)} copy-done((bf16[4,16,3072]{2,1,0:T(8,128)(2,1)S(1)}, bf16[4,16,3072]{2,1,0:T(8,128)(2,1)}, u32[]{:S(2)}) %copy-start) | copy-done | bytes 393240
  1.0 0.0 copy-start.1
  1.0 1.0 %copy-done.1 = bf16[4,16,3072]{2,1,0:T(8,128)(2,1)S(1)} copy-done((bf16[4,16,3072]{2,1,0:T(8,128)(2,1)S(1)}, bf16[4,16,3072]{2,1,0:T(8,128)(2,1)}, u32[]{:S(2)}) %copy-start.1) | copy-done | bytes 393240
  2.0 0.0 copy-start.2
  2.0 1.0 %copy-done.2 = bf16[4,16,3072]{2,1,0:T(8,128)(2,1)S(1)} copy-done((bf16[4,16,3072]{2,1,0:T(8,128)(2,1)S(1)}, bf16[4,16,3072]{2,1,0:T(8,128)(2,1)}, u32[]{:S(2)}) %copy-start.2) | copy-done | bytes 393240
  3.0 0.0 copy-start.3
  3.0 0.7 %copy-done.3 = s32[16,32]{1,0:T(8,128)S(1)} copy-done((s32[16,32]{1,0:T(8,128)S(1)}, s32[16,32]{1,0:T(8,128)}, u32[]{:S(2)}) %copy-start.3) | copy-done | bytes 2072
  3.7 0.0 copy-start.4
  3.7 0.7 %copy-done.4 = s32[16]{0:T(128)S(1)} copy-done((s32[16]{0:T(128)S(1)}, s32[16]{0:T(128)}, u32[]{:S(2)}) %copy-start.4) | copy-done | bytes 88
  4.3 46.8 %shard_map.55 = bf16[4,16,3072]{2,1,0:T(8,128)(2,1)S(1)} custom-call(bf16[4,16,3072]{2,1,0:T(8,128)(2,1)S(1)} %copy-done, bf16[4,16,3072]{2,1,0:T(8,128)(2,1)S(1)} %copy-done.1, bf16[4,16,3072]{2,1,0:T(8,128)(2,1)S(1)} %copy-done.2, s32[16,32]{1,0:T(8,128)S(1)} %copy-done.3, s32[16]{0:T(128)S(1)} %copy-done.4), custom_call_target="tpu_custom_call" | custom-call | tf_op jit(solution)/shard_map/pallas_call | solution.py:340
  51.2 0.7 %copy.7 = bf16[4,16,3072]{2,1,0:T(8,128)(2,1)} copy(bf16[4,16,3072]{2,1,0:T(8,128)(2,1)S(1)} %shard_map.55) | data formatting | bytes 786432
Async XLA Ops:
  0.0 1.0 %copy-start = (bf16[4,16,3072]{2,1,0:T(8,128)(2,1)S(1)}, bf16[4,16,3072]{2,1,0:T(8,128)(2,1)}, u32[]{:S(2)}) copy-start(bf16[4,16,3072]{2,1,0:T(8,128)(2,1)} %query_ref.1) | copy-start | bytes 1179652
  1.0 1.0 %copy-start.1 = (bf16[4,16,3072]{2,1,0:T(8,128)(2,1)S(1)}, bf16[4,16,3072]{2,1,0:T(8,128)(2,1)}, u32[]{:S(2)}) copy-start(bf16[4,16,3072]{2,1,0:T(8,128)(2,1)} %key_ref.1) | copy-start | bytes 1179652
  2.0 1.0 %copy-start.2 = (bf16[4,16,3072]{2,1,0:T(8,128)(2,1)S(1)}, bf16[4,16,3072]{2,1,0:T(8,128)(2,1)}, u32[]{:S(2)}) copy-start(bf16[4,16,3072]{2,1,0:T(8,128)(2,1)} %value_ref.1) | copy-start | bytes 1179652
  3.0 0.7 %copy-start.3 = (s32[16,32]{1,0:T(8,128)S(1)}, s32[16,32]{1,0:T(8,128)}, u32[]{:S(2)}) copy-start(s32[16,32]{1,0:T(8,128)} %pair_ref.1) | copy-start | bytes 6148
  3.7 0.7 %copy-start.4 = (s32[16]{0:T(128)S(1)}, s32[16]{0:T(128)}, u32[]{:S(2)}) copy-start(s32[16]{0:T(128)} %tokens_ref.1) | copy-start | bytes 196
where the time goes:
time: 52.2 us; the launch traced here: 51.9 us
  Pallas kernels  46.8 us (90%)
  local copies, waits for them, and re-layouts  5.09 us (10%)
    pallas_call x1, Pallas kernels, shards(): pl.pallas_call(functools.partial(kernel, sizes), out_shape=jax.ShapeDtype...  46.8 us
    unnamed x11, local copies, waits for them, and re-layouts  5.09 us

commit v1 on v0

--- a/solution.py
+++ b/solution.py
@@ -39,13 +39,14 @@
     key_ref,
     value_ref,
     pair_ref,
-    tokens_ref,
+    tokens_far,
     out_ref,
     gathered,
     store,
     outbox,
     staged,
     pair_here,
+    tokens_ref,
     listed_ref,
     place_ref,
     wanted_ref,
@@ -60,6 +61,7 @@
     back_recv,
     back_local,
     pair_sem,
+    tokens_sem,
 ):
     count_head, count_tm, blocks, part, heads, block, total_blocks, slots, padded = sizes
     width = heads * HD
@@ -155,6 +157,8 @@
         )
     pair_copy = pltpu.make_async_copy(pair_ref, pair_here, pair_sem)
     pair_copy.start()
+    tokens_copy = pltpu.make_async_copy(tokens_far, tokens_ref, tokens_sem)
+    tokens_copy.start()
     for which in range(3):
 
         def start_local(h, carry, which=which):
@@ -174,6 +178,7 @@
         lax.fori_loop(0, heads, start_remote, 0)
 
     pair_copy.wait()
+    tokens_copy.wait()
     pairs = pair_here[...]
     lane = lax.broadcasted_iota(jnp.int32, (1, LANES), 1)
     listed = jnp.zeros((total_blocks, LANES), jnp.float32)
@@ -335,19 +340,20 @@
     shard_rows = -(-count_tm // 8) * 8
     sizes = (count_head, count_tm, blocks, part, heads, block, total_blocks, slots, padded)
     peers = max(1, count_head - 1)
-    anywhere = pl.BlockSpec(memory_space=pl.ANY)
+    in_hbm = pl.BlockSpec(memory_space=pltpu.HBM)
     dma = pltpu.SemaphoreType.DMA
     return pl.pallas_call(
         functools.partial(kernel, sizes),
         out_shape=jax.ShapeDtypeStruct(query_rows.shape, jnp.bfloat16),
-        in_specs=[anywhere] * 4 + [pl.BlockSpec(memory_space=pltpu.SMEM)],
-        out_specs=anywhere,
+        in_specs=[in_hbm] * 5,
+        out_specs=in_hbm,
         scratch_shapes=[
             pltpu.VMEM((3, heads, count_head, blocks, part, HD), jnp.bfloat16),
             pltpu.VMEM((2, heads, padded, block, HD), jnp.bfloat16),
             pltpu.VMEM((2, heads, len(slots), block, HD), jnp.bfloat16),
             pltpu.VMEM((heads, count_head, blocks, part, HD), jnp.bfloat16),
             pltpu.VMEM((total_blocks, listed), jnp.int32),
+            pltpu.SMEM((total_blocks,), jnp.int32),
             pltpu.VMEM((count_tm, blocks, LANES), jnp.float32),
             pltpu.VMEM((NEAR_CAP, count_tm, 1, LANES), jnp.float32),
             pltpu.VMEM((shard_rows, LANES), jnp.float32),
@@ -362,9 +368,10 @@
             dma((peers, heads)),
             dma((heads,)),
             dma(()),
+            dma(()),
         ],
         compiler_params=pltpu.CompilerParams(
-            collective_id=0, has_side_effects=True, vmem_limit_bytes=32 * 1024 * 1024
+            collective_id=0, has_side_effects=True, vmem_limit_bytes=67_043_328
         ),
     )(query_rows, key_rows, value_rows, pair_list, block_tokens)
 

time: 52.2 us -> 48.5 us (0.929)
  local copies, waits for them, and re-layouts: 5.09 us -> 1.77 us
    unnamed x11 -> x1, local copies, waits for them, and re-layouts: 5.09 us -> 1.77 us
where the time goes in v1:
time: 48.5 us; the launch traced here: 48.3 us
  Pallas kernels  46.6 us (96%)
  local copies, waits for them, and re-layouts  1.77 us (4%)
    pallas_call x1, Pallas kernels, shards(): pl.pallas_call(functools.partial(kernel, sizes), out_shape=jax.ShapeDtype...  46.6 us
    unnamed x1, local copies, waits for them, and re-layouts  1.77 us

profile of v1, /device:TPU:0, one launch (start us, length us, event | category | flops | bytes accessed | tf_op | source)
XLA Modules:
  0.0 48.3 jit_solution(6572790686521583212)
XLA Ops:
  0.0 46.6 %shard_map.55 = bf16[4,16,3072]{2,1,0:T(8,128)(2,1)} custom-call(bf16[4,16,3072]{2,1,0:T(8,128)(2,1)} %query_ref.1, bf16[4,16,3072]{2,1,0:T(8,128)(2,1)} %key_ref.1, bf16[4,16,3072]{2,1,0:T(8,128)(2,1)} %value_ref.1, s32[16,32]{1,0:T(8,128)} %pair_ref.1, s32[16]{0:T(128)} %tokens_far.1), custom_call_target="tpu_custom_call" | custom-call | tf_op jit(solution)/shard_map/pallas_call | solution.py:345
  46.6 1.8 %copy.7 = bf16[4,16,3072]{2,1,0:T(8,128)(2,1)} copy(bf16[4,16,3072]{2,1,0:T(8,128)(2,1)} %shard_map.55) | data formatting | bytes 786432

commit v2 on v1

--- a/solution.py
+++ b/solution.py
@@ -159,23 +159,23 @@
     pair_copy.start()
     tokens_copy = pltpu.make_async_copy(tokens_far, tokens_ref, tokens_sem)
     tokens_copy.start()
-    for which in range(3):
-
-        def start_local(h, carry, which=which):
+
+    def start_local(h, carry):
+        for which in range(3):
             local_copy(which, h).start()
-            return carry
-
-        lax.fori_loop(0, heads, start_local, 0)
+        return carry
+
+    lax.fori_loop(0, heads, start_local, 0)
     sign_ref[...] = sign_table(HD).astype(jnp.bfloat16)
     pl.semaphore_wait(pltpu.get_barrier_semaphore(), count_head - 1 + count_tm - 1)
-    for which in range(3):
-
-        def start_remote(h, carry, which=which):
+
+    def start_remote(h, carry):
+        for which in range(3):
             for offset in range(1, count_head):
                 head_copy(which, offset, h).start()
-            return carry
-
-        lax.fori_loop(0, heads, start_remote, 0)
+        return carry
+
+    lax.fori_loop(0, heads, start_remote, 0)
 
     pair_copy.wait()
     tokens_copy.wait()
@@ -247,9 +247,8 @@
         turned = jnp.dot(rows, sign_ref[...], preferred_element_type=jnp.float32) * scale
         return turned.astype(jnp.bfloat16)
 
-    for which in range(2):
-
-        def spread(h, carry, which=which):
+    def spread(h):
+        for which in range(2):
             turned = arrived(which, h)
             store[which, h, 0:blocks] = turned.reshape(blocks, block, HD)
             wide = turned.astype(jnp.float32)
@@ -259,14 +258,11 @@
                     sent = sent + picks[i][j] * wide[j * block : (j + 1) * block]
                 outbox[which, h, i] = sent.astype(jnp.bfloat16)
             for slot in slots:
-                if_used(slot, lambda slot=slot: halo_copy(which, h, slot).start())
-            return carry
-
-        lax.fori_loop(0, heads, spread, 0)
+                if_used(slot, lambda slot=slot, which=which: halo_copy(which, h, slot).start())
 
     position = lax.broadcasted_iota(jnp.int32, (block, HD), 0)
 
-    def attend(h, carry):
+    def attend(h):
         query = arrived(2, h)
         for which in range(2):
             for slot in slots:
@@ -307,9 +303,13 @@
         for offset in range(1, count_head):
             back_copy(offset, h).start()
         back_own(h).start()
+
+    def step(h, carry):
+        pl.when(h < heads)(lambda: spread(h))
+        pl.when(h >= 1)(lambda: attend(h - 1))
         return carry
 
-    lax.fori_loop(0, heads, attend, 0)
+    lax.fori_loop(0, heads + 1, step, 0)
 
     def finish(h, carry):
         for which in range(3):
@@ -371,9 +371,9 @@
             dma(()),
         ],
         compiler_params=pltpu.CompilerParams(
-            collective_id=0, has_side_effects=True, vmem_limit_bytes=67_043_328
+            collective_id=0, has_side_effects=True, vmem_limit_bytes=32 * 1024 * 1024
         ),
-    )(query_rows, key_rows, value_rows, pair_list, block_tokens)
+    )(*[pltpu.with_memory_space_constraint(x, pltpu.HBM) for x in (query_rows, key_rows, value_rows, pair_list, block_tokens)])
 
 
 def solution(mesh):

time: 48.5 us -> 46.9 us (0.967)
  local copies, waits for them, and re-layouts: 1.77 us -> 0.75 us
  Pallas kernels: 46.6 us -> 46 us
    unnamed x1, local copies, waits for them, and re-layouts: 1.77 us -> 0.75 us
    pallas_call x1, Pallas kernels: 46.6 us -> 46 us  [shards(): pl.pallas_call(functools.partial(kernel, sizes), out_shape=jax.ShapeDtype...]
where the time goes in v2:
time: 46.9 us; the launch traced here: 46.8 us
  Pallas kernels  46 us (98%)
  local copies, waits for them, and re-layouts  0.75 us (2%)
    pallas_call x1, Pallas kernels, shards(): pl.pallas_call(functools.partial(kernel, sizes), out_shape=jax.ShapeDtype...  46 us

profile of v2, /device:TPU:0, one launch (start us, length us, event | category | flops | bytes accessed | tf_op | source)
XLA Modules:
  0.0 46.8 jit_solution(9990906496522344680)
XLA Ops:
  0.0 46.0 %shard_map.55 = bf16[4,16,3072]{2,1,0:T(8,128)(2,1)S(1)} custom-call(bf16[4,16,3072]{2,1,0:T(8,128)(2,1)} %query_ref.1, bf16[4,16,3072]{2,1,0:T(8,128)(2,1)} %key_ref.1, bf16[4,16,3072]{2,1,0:T(8,128)(2,1)} %value_ref.1, s32[16,32]{1,0:T(8,128)} %pair_ref.1, s32[16]{0:T(128)} %tokens_far.1), custom_call_target="tpu_custom_call" | custom-call | tf_op jit(solution)/shard_map/pallas_call | solution.py:345
  46.0 0.7 %copy.7 = bf16[4,16,3072]{2,1,0:T(8,128)(2,1)} copy(bf16[4,16,3072]{2,1,0:T(8,128)(2,1)S(1)} %shard_map.55) | data formatting | bytes 786432

commit v3 on v2

--- a/solution.py
+++ b/solution.py
@@ -169,13 +169,20 @@
     sign_ref[...] = sign_table(HD).astype(jnp.bfloat16)
     pl.semaphore_wait(pltpu.get_barrier_semaphore(), count_head - 1 + count_tm - 1)
 
-    def start_remote(h, carry):
-        for which in range(3):
-            for offset in range(1, count_head):
-                head_copy(which, offset, h).start()
+    def start_remote(which, h):
+        for offset in range(1, count_head):
+            head_copy(which, offset, h).start()
+
+    def start_step(h, carry):
+        @pl.when(h < heads)
+        def _():
+            start_remote(0, h)
+            start_remote(1, h)
+
+        pl.when(h >= 1)(lambda: start_remote(2, h - 1))
         return carry
 
-    lax.fori_loop(0, heads, start_remote, 0)
+    lax.fori_loop(0, heads + 1, start_step, 0)
 
     pair_copy.wait()
     tokens_copy.wait()
@@ -269,23 +276,20 @@
                 if_used(slot, lambda slot=slot, which=which: halo_arrival(which, h, slot).wait_recv())
         keys = store[0, h].reshape(padded * block, HD)
         values = store[1, h].reshape(padded * block, HD)
-        mixed = []
+        scores = lax.dot_general(
+            query, keys, (((1,), (1,)), ((), ())), preferred_element_type=jnp.float32
+        )
+        halves, denominators = [], []
         for b in range(blocks):
-            scores = lax.dot_general(
-                query[b * block : (b + 1) * block],
-                keys,
-                (((1,), (1,)), ((), ())),
-                preferred_element_type=jnp.float32,
-            )
-            scores = scores * scale + bias_ref[b : b + 1, :]
-            peak = jnp.max(scores, axis=1, keepdims=True)
-            weights = jnp.exp(scores - peak)
-            denominator = jnp.sum(weights, axis=1, keepdims=True)
-            total = jnp.dot(
-                weights.astype(jnp.bfloat16), values, preferred_element_type=jnp.float32
-            )
-            mixed.append(total / denominator)
-        mixed = jnp.concatenate(mixed, axis=0)
+            of_block = scores[b * block : (b + 1) * block] * scale + bias_ref[b : b + 1, :]
+            peak = jnp.max(of_block, axis=1, keepdims=True)
+            weights = jnp.exp(of_block - peak)
+            denominators.append(jnp.sum(weights, axis=1, keepdims=True))
+            halves.append(weights.astype(jnp.bfloat16))
+        mixed = jnp.dot(
+            jnp.concatenate(halves, axis=0), values, preferred_element_type=jnp.float32
+        )
+        mixed = mixed / jnp.concatenate(denominators, axis=0)
         first = mixed.astype(jnp.bfloat16)
         rest = mixed - first.astype(jnp.float32)
         second = rest.astype(jnp.bfloat16)

time: 46.9 us -> 45.4 us (0.968)
  Pallas kernels: 46 us -> 44.5 us
    pallas_call x1, Pallas kernels: 46 us -> 44.5 us  [shards(): pl.pallas_call(functools.partial(kernel, sizes), out_shape=jax.ShapeDtype...]
where the time goes in v3:
time: 45.4 us; the launch traced here: 45.2 us
  Pallas kernels  44.5 us (98%)
  local copies, waits for them, and re-layouts  0.75 us (2%)
    pallas_call x1, Pallas kernels, shards(): pl.pallas_call(functools.partial(kernel, sizes), out_shape=jax.ShapeDtype...  44.5 us

profile of v3, /device:TPU:0, one launch (start us, length us, event | category | flops | bytes accessed | tf_op | source)
XLA Modules:
  0.0 45.2 jit_solution(4396778147737253206)
XLA Ops:
  0.0 44.5 %shard_map.55 = bf16[4,16,3072]{2,1,0:T(8,128)(2,1)S(1)} custom-call(bf16[4,16,3072]{2,1,0:T(8,128)(2,1)} %query_ref.1, bf16[4,16,3072]{2,1,0:T(8,128)(2,1)} %key_ref.1, bf16[4,16,3072]{2,1,0:T(8,128)(2,1)} %value_ref.1, s32[16,32]{1,0:T(8,128)} %pair_ref.1, s32[16]{0:T(128)} %tokens_far.1), custom_call_target="tpu_custom_call" | custom-call | tf_op jit(solution)/shard_map/pallas_call | solution.py:349
  44.5 0.7 %copy.7 = bf16[4,16,3072]{2,1,0:T(8,128)(2,1)} copy(bf16[4,16,3072]{2,1,0:T(8,128)(2,1)S(1)} %shard_map.55) | data formatting | bytes 786432

commit v4 on v3

--- a/solution.py
+++ b/solution.py
@@ -12,6 +12,7 @@
 NEAR_CAP = 2
 FAR_CAP = 1
 LANES = 128
+LEAD = 2
 MESH = pl.DeviceIdType.MESH
 
 
@@ -21,6 +22,16 @@
         capacity = NEAR_CAP if offset in (1, count_tm - 1) else FAR_CAP
         slots += [(offset, place) for place in range(capacity)]
     return slots
+
+
+def partner(index, offset, count):
+    if count & (count - 1):
+        return lax.rem(index + offset, count)
+    for level in range(count.bit_length() - 1):
+        if offset >> level & 1:
+            bit = lax.rem(lax.div(index, 1 << level), 2)
+            index = index + (1 << level) * (1 - 2 * bit)
+    return index
 
 
 def sign_table(dimension):
@@ -71,8 +82,8 @@
     slot_of = {slot: i for i, slot in enumerate(slots)}
     sources = (key_ref, value_ref, query_ref)
 
-    for offset in range(1, count_head):
-        peer = lax.rem(my_head + offset, count_head)
+    for offset in reversed(range(1, count_head)):
+        peer = partner(my_head, offset, count_head)
         pl.semaphore_signal(
             pltpu.get_barrier_semaphore(), inc=1, device_id={"head": peer}, device_id_type=MESH
         )
@@ -81,7 +92,7 @@
         return pl.ds(pl.multiple_of(owner * width + h * HD, HD), HD)
 
     def head_copy(which, offset, h):
-        peer = lax.rem(my_head + offset, count_head)
+        peer = partner(my_head, offset, count_head)
         return pltpu.make_async_remote_copy(
             src_ref=sources[which].at[:, :, columns_of(peer, h)],
             dst_ref=gathered.at[which, h, my_head],
@@ -132,7 +143,7 @@
             pl.when(near)(action)
 
     def back_copy(offset, h):
-        peer = lax.rem(my_head + offset, count_head)
+        peer = partner(my_head, offset, count_head)
         return pltpu.make_async_remote_copy(
             src_ref=staged.at[h, peer],
             dst_ref=out_ref.at[:, :, columns_of(my_head, h)],
@@ -160,17 +171,11 @@
     tokens_copy = pltpu.make_async_copy(tokens_far, tokens_ref, tokens_sem)
     tokens_copy.start()
 
-    def start_local(h, carry):
-        for which in range(3):
-            local_copy(which, h).start()
-        return carry
-
-    lax.fori_loop(0, heads, start_local, 0)
     sign_ref[...] = sign_table(HD).astype(jnp.bfloat16)
     pl.semaphore_wait(pltpu.get_barrier_semaphore(), count_head - 1 + count_tm - 1)
 
     def start_remote(which, h):
-        for offset in range(1, count_head):
+        for offset in reversed(range(1, count_head)):
             head_copy(which, offset, h).start()
 
     def start_step(h, carry):
@@ -179,10 +184,17 @@
             start_remote(0, h)
             start_remote(1, h)
 
-        pl.when(h >= 1)(lambda: start_remote(2, h - 1))
+        pl.when(h >= LEAD)(lambda: start_remote(2, h - LEAD))
         return carry
 
-    lax.fori_loop(0, heads + 1, start_step, 0)
+    lax.fori_loop(0, heads + LEAD, start_step, 0)
+
+    def start_local(h, carry):
+        for which in range(3):
+            local_copy(which, h).start()
+        return carry
+
+    lax.fori_loop(0, heads, start_local, 0)
 
     pair_copy.wait()
     tokens_copy.wait()
@@ -242,7 +254,7 @@
 
     def arrived(which, h):
         local_copy(which, h).wait()
-        for offset in range(1, count_head):
+        for offset in reversed(range(1, count_head)):
             head_copy(which, offset, h).wait_recv()
         rows = jnp.concatenate(
             [
@@ -295,8 +307,11 @@
         second = rest.astype(jnp.bfloat16)
         third = (rest - second.astype(jnp.float32)).astype(jnp.bfloat16)
         sign = sign_ref[...]
-        turned = jnp.dot(first, sign, preferred_element_type=jnp.float32)
-        turned = turned + jnp.dot(second, sign, preferred_element_type=jnp.float32)
+        turned = jnp.dot(
+            jnp.concatenate([first, second], axis=1),
+            jnp.concatenate([sign, sign], axis=0),
+            preferred_element_type=jnp.float32,
+        )
         turned = turned + jnp.dot(third, sign, preferred_element_type=jnp.float32)
         turned = turned * scale
         for b in range(blocks):
@@ -304,25 +319,25 @@
             result = jnp.where(live, turned[b * block : (b + 1) * block], 0.0)
             for owner in range(count_head):
                 staged[h, owner, b] = result[owner * part : (owner + 1) * part].astype(jnp.bfloat16)
-        for offset in range(1, count_head):
+        for offset in reversed(range(1, count_head)):
             back_copy(offset, h).start()
         back_own(h).start()
 
     def step(h, carry):
         pl.when(h < heads)(lambda: spread(h))
-        pl.when(h >= 1)(lambda: attend(h - 1))
+        pl.when(h >= LEAD)(lambda: attend(h - LEAD))
         return carry
 
-    lax.fori_loop(0, heads + 1, step, 0)
+    lax.fori_loop(0, heads + LEAD, step, 0)
 
     def finish(h, carry):
         for which in range(3):
-            for offset in range(1, count_head):
+            for offset in reversed(range(1, count_head)):
                 head_copy(which, offset, h).wait_send()
         for which in range(2):
             for slot in slots:
                 if_used(slot, lambda slot=slot, which=which: halo_copy(which, h, slot).wait_send())
-        for offset in range(1, count_head):
+        for offset in reversed(range(1, count_head)):
             back_copy(offset, h).wait()
         back_own(h).wait()
         return carry

time: 45.4 us -> 44 us (0.969)
  Pallas kernels: 44.5 us -> 43.1 us
    pallas_call x1, Pallas kernels: 44.5 us -> 43.1 us  [shards(): pl.pallas_call(functools.partial(kernel, sizes), out_shape=jax.ShapeDtype...]
where the time goes in v4:
time: 44 us; the launch traced here: 43.9 us
  Pallas kernels  43.1 us (98%)
  local copies, waits for them, and re-layouts  0.75 us (2%)
    pallas_call x1, Pallas kernels, shards(): pl.pallas_call(functools.partial(kernel, sizes), out_shape=jax.ShapeDtype...  43.1 us

profile of v4, /device:TPU:0, one launch (start us, length us, event | category | flops | bytes accessed | tf_op | source)
XLA Modules:
  0.0 43.9 jit_solution(4529268935834070542)
XLA Ops:
  0.0 43.1 %shard_map.55 = bf16[4,16,3072]{2,1,0:T(8,128)(2,1)S(1)} custom-call(bf16[4,16,3072]{2,1,0:T(8,128)(2,1)} %query_ref.1, bf16[4,16,3072]{2,1,0:T(8,128)(2,1)} %key_ref.1, bf16[4,16,3072]{2,1,0:T(8,128)(2,1)} %value_ref.1, s32[16,32]{1,0:T(8,128)} %pair_ref.1, s32[16]{0:T(128)} %tokens_far.1), custom_call_target="tpu_custom_call" | custom-call | tf_op jit(solution)/shard_map/pallas_call | solution.py:364
  43.1 0.7 %copy.7 = bf16[4,16,3072]{2,1,0:T(8,128)(2,1)} copy(bf16[4,16,3072]{2,1,0:T(8,128)(2,1)S(1)} %shard_map.55) | data formatting | bytes 786432
